TPU v7x, 32 devices: a whole 2x2x4 slice. The times are simulated.
32 devices in a mesh: people: 8 (over z, x), snps: 4 (over y, core).
Axes of the slice: x: 2, y: 2, z: 4, core: 2. Of those that a mesh axis runs over, the one named last changes fastest.
Arguments:
- genotype: bfloat16 [4096, 16384], P('people', 'snps'), may hold values from 0 to 2, as said below
- residual_init: float32 [32, 4096], P(None, 'people'), may hold values from -30 to 30
- effects_init: float32 [32, 16384], P(None, 'snps'), may hold values from -3 to 3
- allele_freq: float32 [16384], P('snps'), may hold values from 0.05 to 0.5, as said below
- snp_scale: float32 [16384], P('snps'), may hold values from 0.8 to 1.25
- ld_basis: bfloat16 [32, 512, 512], P('snps'), may hold values from -1 to 1, as said below
- ld_eig: float32 [16384], P('snps'), may hold values from 0.5 to 2
- ridge: float32 [32], replicated, may hold values from 1.5 to 4
- noise_scale: float32 [32], replicated, may hold values from 0.2 to 1
- normal_draws: bfloat16 [4, 32, 16384], P(None, None, 'snps'), may hold values from -5 to 5
- assignment: int32 [32], P('snps'), may hold values from 0 to 7, as said below
Outputs:
- effects: float32 [32, 16384], P(None, 'snps')
- residual: float32 [32, 4096], P(None, 'people')
Inputs may be any that keep to these rules, and one draw needn't show every extreme that they name: `assignment`: the 8 entries that lie on one index of snps are each a permutation of 0 to 7. `ld_basis`: each block's basis is orthogonal up to its rounding to bfloat16. `genotype`: only the values 0, 1 and 2 occur; each dosage counts two alleles, each present with the SNP's allele_freq. `allele_freq`: multiples of 0.001.
All inputs are finite; a program needn't handle non-finite values.
Results may differ from a plain program's by a relative error of at most 0.014.
Values sent between devices are 32-bit elements; how exact they have to be, the bound alone decides.
A program may use at most 64 MiB of HBM per device.

v0:
```python
import jax
import jax.numpy as jnp
from jax import lax
from jax.sharding import PartitionSpec as P

WINDOW = 4
GROUPS_DEV = 2


def contract_last(left, right):
    return lax.dot_general(
        left, right, (((1,), (1,)), ((), ())), preferred_element_type=jnp.float32
    )


def sum_block(stacked):
    return lax.psum(stacked, "people")


def sample_block(summed_row, old_effects, block_basis, block_eig, draws_block, spread, ridge):
    prior = jnp.dot(
        old_effects.astype(jnp.bfloat16), block_basis, preferred_element_type=jnp.float32
    )
    coupled = contract_last((prior * block_eig[None, :]).astype(jnp.bfloat16), block_basis)
    rotated = jnp.dot(
        (summed_row + coupled).astype(jnp.bfloat16), block_basis, preferred_element_type=jnp.float32
    )
    precision = block_eig[None, :] + ridge[:, None]
    sampled = rotated / precision + spread[:, None] * draws_block.astype(jnp.float32) / jnp.sqrt(
        precision
    )
    return contract_last(sampled.astype(jnp.bfloat16), block_basis)


def per_device(
    genotype,
    residual_init,
    effects_init,
    allele_freq,
    snp_scale,
    ld_basis,
    ld_eig,
    ridge,
    noise_scale,
    normal_draws,
    assignment,
):
    block_width = ld_basis.shape[1]
    people_total = genotype.shape[0] * lax.axis_size("people")
    col_scale = snp_scale / jnp.sqrt(people_total * 2.0 * allele_freq * (1.0 - allele_freq))
    residual = residual_init
    effects = effects_init
    for round_idx in range(normal_draws.shape[0]):
        start_residual = residual
        local_squares = jnp.sum(residual * residual, axis=1)
        spread = None
        sum_squares = lax.psum(local_squares, "people")
        spread = noise_scale * jnp.sqrt(sum_squares / people_total + 1e-06)
        states = [residual for member in range(GROUPS_DEV)]
        plan = [[(member, slot_idx)] for member in range(GROUPS_DEV) for slot_idx in range(WINDOW)]
        for step_index, members in enumerate(plan):
            prepared = []
            partials = []
            for member, slot_idx in members:
                local_block = assignment[member * WINDOW + slot_idx]
                col_start = local_block * block_width
                block_x = lax.dynamic_slice_in_dim(genotype, col_start, block_width, 1)
                block_freq = lax.dynamic_slice_in_dim(allele_freq, col_start, block_width, 0)
                block_scale = lax.dynamic_slice_in_dim(col_scale, col_start, block_width, 0)
                state = states[member]
                cross_term = jnp.dot(
                    state.astype(jnp.bfloat16), block_x, preferred_element_type=jnp.float32
                )
                partial_value = block_scale[None, :] * (
                    cross_term - 2.0 * block_freq[None, :] * jnp.sum(state, axis=1)[:, None]
                )
                partials.append(partial_value)
                prepared.append((member, local_block, col_start, block_x, block_freq, block_scale))
            stacked = jnp.stack(partials, axis=0)
            summed = sum_block(stacked)
            for position, entry in enumerate(prepared):
                member, local_block, col_start, block_x, block_freq, block_scale = entry
                block_basis = lax.dynamic_index_in_dim(ld_basis, local_block, 0, keepdims=False)
                block_eig = lax.dynamic_slice_in_dim(ld_eig, col_start, block_width, 0)
                old_effects = lax.dynamic_slice_in_dim(effects, col_start, block_width, 1)
                draws_block = lax.dynamic_slice_in_dim(
                    normal_draws[round_idx], col_start, block_width, 1
                )
                fresh = sample_block(
                    summed[position],
                    old_effects,
                    block_basis,
                    block_eig,
                    draws_block,
                    spread,
                    ridge,
                )
                change = fresh - old_effects
                effects = lax.dynamic_update_slice_in_dim(effects, fresh, col_start, 1)
                weighted = change * block_scale[None, :]
                shift_term = 2.0 * jnp.sum(weighted * block_freq[None, :], axis=1)
                states[member] = (
                    states[member]
                    - contract_last(weighted.astype(jnp.bfloat16), block_x)
                    + shift_term[:, None]
                )
        local_changes = states[0] - start_residual
        member = 1
        local_changes = local_changes + (states[member] - start_residual)
        residual = start_residual + lax.psum(local_changes, "snps")
    return (effects, residual)


def solution(mesh):
    return jax.shard_map(
        per_device,
        mesh=mesh,
        in_specs=(
            P("people", "snps"),
            P(None, "people"),
            P(None, "snps"),
            P("snps"),
            P("snps"),
            P("snps", None, None),
            P("snps"),
            P(),
            P(),
            P(None, None, "snps"),
            P("snps"),
        ),
        out_specs=(P(None, "snps"), P(None, "people")),
        check_vma=False,
    )
```

profile of v0, /device:TPU:0, one launch (start us, length us, event | category | flops | bytes accessed | tf_op | source)
XLA Modules:
  0.0 2370.5 jit_solution(16344473810487242396)
XLA Ops:
  62.1 28.9 %all-reduce.37.cloned.1.call-done = f32[32,512]{1,0:T(8,128)} async-done(((f32[32,512]{1,0:T(8,128)}), f32[32,512]{1,0:T(8,128)}) %all-reduce.37.cloned.1.call-update) | async-done | bytes 65552 | tf_op jit(solution)/shard_map/psum | solution.py:17
  98.9 67.9 %all-reduce.39.cloned.1.call-done = f32[32,512]{1,0:T(8,128)} async-done(((f32[32,512]{1,0:T(8,128)}), f32[32,512]{1,0:T(8,128)}) %all-reduce.39.cloned.1.call-update) | async-done | bytes 65552 | tf_op jit(solution)/shard_map/psum | solution.py:17
  174.7 68.1 %all-reduce.41.cloned.1.call-done = f32[32,512]{1,0:T(8,128)} async-done(((f32[32,512]{1,0:T(8,128)}), f32[32,512]{1,0:T(8,128)}) %all-reduce.41.cloned.1.call-update) | async-done | bytes 65552 | tf_op jit(solution)/shard_map/psum | solution.py:17
  250.6 69.5 %all-reduce.99.cloned.1.call-done = (f32[32,512]{1,0:T(8,128)}, f32[32,512]{1,0:T(8,128)}) async-done(((f32[32,512]{1,0:T(8,128)}, f32[32,512]{1,0:T(8,128)}), (f32[32,512]{1,0:T(8,128)}, f32[32,512]{1,0:T(8,128)})) %all-reduce.99.cloned.1.call-update) | async-done | bytes 131088 | tf_op jit(solution)/shard_map/psum | solution.py:17
  332.8 66.7 %all-reduce.43.cloned.1.call-done = f32[32,512]{1,0:T(8,128)} async-done(((f32[32,512]{1,0:T(8,128)}), f32[32,512]{1,0:T(8,128)}) %all-reduce.43.cloned.1.call-update) | async-done | bytes 65552 | tf_op jit(solution)/shard_map/psum | solution.py:17
  407.3 68.0 %all-reduce.45.cloned.1.call-done = f32[32,512]{1,0:T(8,128)} async-done(((f32[32,512]{1,0:T(8,128)}), f32[32,512]{1,0:T(8,128)}) %all-reduce.45.cloned.1.call-update) | async-done | bytes 65552 | tf_op jit(solution)/shard_map/psum | solution.py:17
  483.1 68.0 %all-reduce.47.cloned.1.call-done = f32[32,512]{1,0:T(8,128)} async-done(((f32[32,512]{1,0:T(8,128)}), f32[32,512]{1,0:T(8,128)}) %all-reduce.47.cloned.1.call-update) | async-done | bytes 65552 | tf_op jit(solution)/shard_map/psum | solution.py:17
  558.9 30.3 %all-reduce.49.cloned.1.call-done = f32[32,512]{1,0:T(8,128)} async-done(((f32[32,512]{1,0:T(8,128)}), f32[32,512]{1,0:T(8,128)}) %all-reduce.49.cloned.1.call-update) | async-done | bytes 65552 | tf_op jit(solution)/shard_map/psum | solution.py:110
  615.4 65.6 %all-reduce.51.cloned.1.call-done = f32[32,512]{1,0:T(8,128)} async-done(((f32[32,512]{1,0:T(8,128)}), f32[32,512]{1,0:T(8,128)}) %all-reduce.51.cloned.1.call-update) | async-done | bytes 65552 | tf_op jit(solution)/shard_map/psum | solution.py:17
  688.9 67.9 %all-reduce.53.cloned.1.call-done = f32[32,512]{1,0:T(8,128)} async-done(((f32[32,512]{1,0:T(8,128)}), f32[32,512]{1,0:T(8,128)}) %all-reduce.53.cloned.1.call-update) | async-done | bytes 65552 | tf_op jit(solution)/shard_map/psum | solution.py:17
  764.6 68.1 %all-reduce.55.cloned.1.call-done = f32[32,512]{1,0:T(8,128)} async-done(((f32[32,512]{1,0:T(8,128)}), f32[32,512]{1,0:T(8,128)}) %all-reduce.55.cloned.1.call-update) | async-done | bytes 65552 | tf_op jit(solution)/shard_map/psum | solution.py:17
  840.6 69.5 %all-reduce.97.cloned.1.call-done = (f32[32,512]{1,0:T(8,128)}, f32[32,512]{1,0:T(8,128)}) async-done(((f32[32,512]{1,0:T(8,128)}, f32[32,512]{1,0:T(8,128)}), (f32[32,512]{1,0:T(8,128)}, f32[32,512]{1,0:T(8,128)})) %all-reduce.97.cloned.1.call-update) | async-done | bytes 131088 | tf_op jit(solution)/shard_map/psum | solution.py:17
  922.3 68.4 %all-reduce.57.cloned.1.call-done = f32[32,512]{1,0:T(8,128)} async-done(((f32[32,512]{1,0:T(8,128)}), f32[32,512]{1,0:T(8,128)}) %all-reduce.57.cloned.1.call-update) | async-done | bytes 65552 | tf_op jit(solution)/shard_map/psum | solution.py:17
  998.7 67.8 %all-reduce.59.cloned.1.call-done = f32[32,512]{1,0:T(8,128)} async-done(((f32[32,512]{1,0:T(8,128)}), f32[32,512]{1,0:T(8,128)}) %all-reduce.59.cloned.1.call-update) | async-done | bytes 65552 | tf_op jit(solution)/shard_map/psum | solution.py:17
  1074.3 68.0 %all-reduce.61.cloned.1.call-done = f32[32,512]{1,0:T(8,128)} async-done(((f32[32,512]{1,0:T(8,128)}), f32[32,512]{1,0:T(8,128)}) %all-reduce.61.cloned.1.call-update) | async-done | bytes 65552 | tf_op jit(solution)/shard_map/psum | solution.py:17
  1150.1 30.3 %all-reduce.63.cloned.1.call-done = f32[32,512]{1,0:T(8,128)} async-done(((f32[32,512]{1,0:T(8,128)}), f32[32,512]{1,0:T(8,128)}) %all-reduce.63.cloned.1.call-update) | async-done | bytes 65552 | tf_op jit(solution)/shard_map/psum | solution.py:110
  1206.5 65.6 %all-reduce.65.cloned.1.call-done = f32[32,512]{1,0:T(8,128)} async-done(((f32[32,512]{1,0:T(8,128)}), f32[32,512]{1,0:T(8,128)}) %all-reduce.65.cloned.1.call-update) | async-done | bytes 65552 | tf_op jit(solution)/shard_map/psum | solution.py:17
  1280.1 67.9 %all-reduce.67.cloned.1.call-done = f32[32,512]{1,0:T(8,128)} async-done(((f32[32,512]{1,0:T(8,128)}), f32[32,512]{1,0:T(8,128)}) %all-reduce.67.cloned.1.call-update) | async-done | bytes 65552 | tf_op jit(solution)/shard_map/psum | solution.py:17
  1355.8 68.1 %all-reduce.69.cloned.1.call-done = f32[32,512]{1,0:T(8,128)} async-done(((f32[32,512]{1,0:T(8,128)}), f32[32,512]{1,0:T(8,128)}) %all-reduce.69.cloned.1.call-update) | async-done | bytes 65552 | tf_op jit(solution)/shard_map/psum | solution.py:17
  1431.7 69.4 %all-reduce.95.cloned.1.call-done = (f32[32,512]{1,0:T(8,128)}, f32[32,512]{1,0:T(8,128)}) async-done(((f32[32,512]{1,0:T(8,128)}, f32[32,512]{1,0:T(8,128)}), (f32[32,512]{1,0:T(8,128)}, f32[32,512]{1,0:T(8,128)})) %all-reduce.95.cloned.1.call-update) | async-done | bytes 131088 | tf_op jit(solution)/shard_map/psum | solution.py:17
  1513.3 68.4 %all-reduce.71.cloned.1.call-done = f32[32,512]{1,0:T(8,128)} async-done(((f32[32,512]{1,0:T(8,128)}), f32[32,512]{1,0:T(8,128)}) %all-reduce.71.cloned.1.call-update) | async-done | bytes 65552 | tf_op jit(solution)/shard_map/psum | solution.py:17
  1589.5 68.0 %all-reduce.73.cloned.1.call-done = f32[32,512]{1,0:T(8,128)} async-done(((f32[32,512]{1,0:T(8,128)}), f32[32,512]{1,0:T(8,128)}) %all-reduce.73.cloned.1.call-update) | async-done | bytes 65552 | tf_op jit(solution)/shard_map/psum | solution.py:17
  1665.3 68.0 %all-reduce.75.cloned.1.call-done = f32[32,512]{1,0:T(8,128)} async-done(((f32[32,512]{1,0:T(8,128)}), f32[32,512]{1,0:T(8,128)}) %all-reduce.75.cloned.1.call-update) | async-done | bytes 65552 | tf_op jit(solution)/shard_map/psum | solution.py:17
  1741.1 30.3 %all-reduce.77.cloned.1.call-done = f32[32,512]{1,0:T(8,128)} async-done(((f32[32,512]{1,0:T(8,128)}), f32[32,512]{1,0:T(8,128)}) %all-reduce.77.cloned.1.call-update) | async-done | bytes 65552 | tf_op jit(solution)/shard_map/psum | solution.py:110
  1797.5 65.6 %all-reduce.79.cloned.1.call-done = f32[32,512]{1,0:T(8,128)} async-done(((f32[32,512]{1,0:T(8,128)}), f32[32,512]{1,0:T(8,128)}) %all-reduce.79.cloned.1.call-update) | async-done | bytes 65552 | tf_op jit(solution)/shard_map/psum | solution.py:17
  1871.0 67.8 %all-reduce.81.cloned.1.call-done = f32[32,512]{1,0:T(8,128)} async-done(((f32[32,512]{1,0:T(8,128)}), f32[32,512]{1,0:T(8,128)}) %all-reduce.81.cloned.1.call-update) | async-done | bytes 65552 | tf_op jit(solution)/shard_map/psum | solution.py:17
  1946.6 68.1 %all-reduce.83.cloned.1.call-done = f32[32,512]{1,0:T(8,128)} async-done(((f32[32,512]{1,0:T(8,128)}), f32[32,512]{1,0:T(8,128)}) %all-reduce.83.cloned.1.call-update) | async-done | bytes 65552 | tf_op jit(solution)/shard_map/psum | solution.py:17
  2022.5 69.5 %all-reduce.93.cloned.1.call-done = (f32[32,512]{1,0:T(8,128)}, f32[32,512]{1,0:T(8,128)}) async-done(((f32[32,512]{1,0:T(8,128)}, f32[32,512]{1,0:T(8,128)}), (f32[32,512]{1,0:T(8,128)}, f32[32,512]{1,0:T(8,128)})) %all-reduce.93.cloned.1.call-update) | async-done | bytes 131088 | tf_op jit(solution)/shard_map/psum | solution.py:17
  2104.2 68.4 %all-reduce.85.cloned.1.call-done = f32[32,512]{1,0:T(8,128)} async-done(((f32[32,512]{1,0:T(8,128)}), f32[32,512]{1,0:T(8,128)}) %all-reduce.85.cloned.1.call-update) | async-done | bytes 65552 | tf_op jit(solution)/shard_map/psum | solution.py:17
  2180.4 68.0 %all-reduce.87.cloned.1.call-done = f32[32,512]{1,0:T(8,128)} async-done(((f32[32,512]{1,0:T(8,128)}), f32[32,512]{1,0:T(8,128)}) %all-reduce.87.cloned.1.call-update) | async-done | bytes 65552 | tf_op jit(solution)/shard_map/psum | solution.py:17
  2256.2 68.0 %all-reduce.89.cloned.1.call-done = f32[32,512]{1,0:T(8,128)} async-done(((f32[32,512]{1,0:T(8,128)}), f32[32,512]{1,0:T(8,128)}) %all-reduce.89.cloned.1.call-update) | async-done | bytes 65552 | tf_op jit(solution)/shard_map/psum | solution.py:17
  2330.8 31.6 %all-reduce.91.cloned.1.call-done = f32[32,512]{1,0:T(8,128)} async-done(((f32[32,512]{1,0:T(8,128)}), f32[32,512]{1,0:T(8,128)}) %all-reduce.91.cloned.1.call-update) | async-done | bytes 65552 | tf_op jit(solution)/shard_map/psum | solution.py:110
  (380 shorter events, 349.0 us)
Async XLA Ops:
  7.2 83.7 %all-reduce.37.cloned.1.call-start = ((), (), s32[]{:S(2)}) async-start(), calls=%async_computation | async-start | bytes 131072 | tf_op jit(solution)/shard_map/psum | solution.py:17
  18.7 148.1 %all-reduce.39.cloned.1.call-start = ((), (), s32[]{:S(2)}) async-start(), calls=%async_computation.1 | async-start | bytes 131072 | tf_op jit(solution)/shard_map/psum | solution.py:17
  97.6 145.2 %all-reduce.41.cloned.1.call-start = ((), (), s32[]{:S(2)}) async-start(), calls=%async_computation.2 | async-start | bytes 131072 | tf_op jit(solution)/shard_map/psum | solution.py:17
  173.3 146.8 %all-reduce.99.cloned.1.call-start = ((), (), s32[]{:S(2)}) async-start(), calls=%async_computation.31 | async-start | bytes 262144 | tf_op jit(solution)/shard_map/psum | solution.py:17
  249.3 150.2 %all-reduce.43.cloned.1.call-start = ((), (), s32[]{:S(2)}) async-start(), calls=%async_computation.3 | async-start | bytes 131072 | tf_op jit(solution)/shard_map/psum | solution.py:17
  331.0 144.3 %all-reduce.45.cloned.1.call-start = ((), (), s32[]{:S(2)}) async-start(), calls=%async_computation.4 | async-start | bytes 131072 | tf_op jit(solution)/shard_map/psum | solution.py:17
  406.0 145.2 %all-reduce.47.cloned.1.call-start = ((), (), s32[]{:S(2)}) async-start(), calls=%async_computation.5 | async-start | bytes 131072 | tf_op jit(solution)/shard_map/psum | solution.py:17
  481.8 107.4 %all-reduce.49.cloned.1.call-start = ((), (), s32[]{:S(2)}) async-start(), calls=%async_computation.6 | async-start | bytes 131072 | tf_op jit(solution)/shard_map/psum | solution.py:110
  557.5 123.4 %all-reduce.51.cloned.1.call-start = ((), (), s32[]{:S(2)}) async-start(), calls=%async_computation.7 | async-start | bytes 131072 | tf_op jit(solution)/shard_map/psum | solution.py:17
  615.3 141.5 %all-reduce.53.cloned.1.call-start = ((), (), s32[]{:S(2)}) async-start(), calls=%async_computation.8 | async-start | bytes 131072 | tf_op jit(solution)/shard_map/psum | solution.py:17
  687.5 145.2 %all-reduce.55.cloned.1.call-start = ((), (), s32[]{:S(2)}) async-start(), calls=%async_computation.9 | async-start | bytes 131072 | tf_op jit(solution)/shard_map/psum | solution.py:17
  763.3 146.8 %all-reduce.97.cloned.1.call-start = ((), (), s32[]{:S(2)}) async-start(), calls=%async_computation.30 | async-start | bytes 262144 | tf_op jit(solution)/shard_map/psum | solution.py:17
  839.3 151.5 %all-reduce.57.cloned.1.call-start = ((), (), s32[]{:S(2)}) async-start(), calls=%async_computation.10 | async-start | bytes 131072 | tf_op jit(solution)/shard_map/psum | solution.py:17
  922.2 144.3 %all-reduce.59.cloned.1.call-start = ((), (), s32[]{:S(2)}) async-start(), calls=%async_computation.11 | async-start | bytes 131072 | tf_op jit(solution)/shard_map/psum | solution.py:17
  997.2 145.2 %all-reduce.61.cloned.1.call-start = ((), (), s32[]{:S(2)}) async-start(), calls=%async_computation.12 | async-start | bytes 131072 | tf_op jit(solution)/shard_map/psum | solution.py:17
  1073.0 107.4 %all-reduce.63.cloned.1.call-start = ((), (), s32[]{:S(2)}) async-start(), calls=%async_computation.13 | async-start | bytes 131072 | tf_op jit(solution)/shard_map/psum | solution.py:110
  1148.7 123.4 %all-reduce.65.cloned.1.call-start = ((), (), s32[]{:S(2)}) async-start(), calls=%async_computation.14 | async-start | bytes 131072 | tf_op jit(solution)/shard_map/psum | solution.py:17
  1206.5 141.5 %all-reduce.67.cloned.1.call-start = ((), (), s32[]{:S(2)}) async-start(), calls=%async_computation.15 | async-start | bytes 131072 | tf_op jit(solution)/shard_map/psum | solution.py:17
  1278.7 145.2 %all-reduce.69.cloned.1.call-start = ((), (), s32[]{:S(2)}) async-start(), calls=%async_computation.16 | async-start | bytes 131072 | tf_op jit(solution)/shard_map/psum | solution.py:17
  1354.4 146.7 %all-reduce.95.cloned.1.call-start = ((), (), s32[]{:S(2)}) async-start(), calls=%async_computation.29 | async-start | bytes 262144 | tf_op jit(solution)/shard_map/psum | solution.py:17
  1430.4 151.4 %all-reduce.71.cloned.1.call-start = ((), (), s32[]{:S(2)}) async-start(), calls=%async_computation.17 | async-start | bytes 131072 | tf_op jit(solution)/shard_map/psum | solution.py:17
  1513.2 144.3 %all-reduce.73.cloned.1.call-start = ((), (), s32[]{:S(2)}) async-start(), calls=%async_computation.18 | async-start | bytes 131072 | tf_op jit(solution)/shard_map/psum | solution.py:17
  1588.2 145.1 %all-reduce.75.cloned.1.call-start = ((), (), s32[]{:S(2)}) async-start(), calls=%async_computation.19 | async-start | bytes 131072 | tf_op jit(solution)/shard_map/psum | solution.py:17
  1663.9 107.4 %all-reduce.77.cloned.1.call-start = ((), (), s32[]{:S(2)}) async-start(), calls=%async_computation.20 | async-start | bytes 131072 | tf_op jit(solution)/shard_map/psum | solution.py:110
  1739.7 123.3 %all-reduce.79.cloned.1.call-start = ((), (), s32[]{:S(2)}) async-start(), calls=%async_computation.21 | async-start | bytes 131072 | tf_op jit(solution)/shard_map/psum | solution.py:17
  1797.4 141.4 %all-reduce.81.cloned.1.call-start = ((), (), s32[]{:S(2)}) async-start(), calls=%async_computation.22 | async-start | bytes 131072 | tf_op jit(solution)/shard_map/psum | solution.py:17
  1869.6 145.1 %all-reduce.83.cloned.1.call-start = ((), (), s32[]{:S(2)}) async-start(), calls=%async_computation.23 | async-start | bytes 131072 | tf_op jit(solution)/shard_map/psum | solution.py:17
  1945.3 146.7 %all-reduce.93.cloned.1.call-start = ((), (), s32[]{:S(2)}) async-start(), calls=%async_computation.28 | async-start | bytes 262144 | tf_op jit(solution)/shard_map/psum | solution.py:17
  2021.2 151.4 %all-reduce.85.cloned.1.call-start = ((), (), s32[]{:S(2)}) async-start(), calls=%async_computation.24 | async-start | bytes 131072 | tf_op jit(solution)/shard_map/psum | solution.py:17
  2104.1 144.3 %all-reduce.87.cloned.1.call-start = ((), (), s32[]{:S(2)}) async-start(), calls=%async_computation.25 | async-start | bytes 131072 | tf_op jit(solution)/shard_map/psum | solution.py:17
  2179.1 145.1 %all-reduce.89.cloned.1.call-start = ((), (), s32[]{:S(2)}) async-start(), calls=%async_computation.26 | async-start | bytes 131072 | tf_op jit(solution)/shard_map/psum | solution.py:17
  2254.8 107.6 %all-reduce.91.cloned.1.call-start = ((), (), s32[]{:S(2)}) async-start(), calls=%async_computation.27 | async-start | bytes 131072 | tf_op jit(solution)/shard_map/psum | solution.py:110
  (37 other events, 5739.3 us)
Sparse Core Ops, SparseCore 0:
  18.8 72.1 all-reduce.36
  97.7 69.0 all-reduce.38
  173.5 69.3 all-reduce.40
  249.4 70.6 all-reduce.98
  331.1 68.3 all-reduce.42
  406.1 69.1 all-reduce.44
  481.9 69.1 all-reduce.46
  557.7 31.4 all-reduce.48
  615.4 65.5 all-reduce.50
  687.7 69.0 all-reduce.52
  763.4 69.3 all-reduce.54
  839.4 70.6 all-reduce.96
  922.3 68.3 all-reduce.56
  997.3 69.1 all-reduce.58
  1073.1 69.1 all-reduce.60
  1148.9 31.4 all-reduce.62
  1206.6 65.5 all-reduce.64
  1278.8 69.0 all-reduce.66
  1354.5 69.3 all-reduce.68
  1430.5 70.5 all-reduce.94
  1513.3 68.3 all-reduce.70
  1588.3 69.1 all-reduce.72
  1664.1 69.2 all-reduce.74
  1739.8 31.4 all-reduce.76
  1797.5 65.4 all-reduce.78
  1869.8 69.0 all-reduce.80
  1945.4 69.2 all-reduce.82
  2021.3 70.6 all-reduce.92
  2104.3 68.3 all-reduce.84
  2179.2 69.1 all-reduce.86
  2255.0 69.2 all-reduce.88
  2330.9 31.4 all-reduce.90
where the time goes:
time: 2380 us; the launch traced here: 2370 us
  waiting for transfers between devices  1990 us (84%)
  matrix products  247 us (10%)
  blocking collectives  87.1 us (4%)
  between operations  35.6 us (1%)
    psum x28, waiting for transfers between devices, sum_block(): return lax.psum(stacked, 'people')  1860 us
    psum x4, waiting for transfers between devices, per_device(): residual = start_residual + lax.psum(local_changes, 'snps')  123 us
    dot_general x64, matrix products, contract_last(): lax.dot_general(left, right, (((1,), (1,)), ((), ())), preferred_element_...  93 us
    psum x4, blocking collectives, per_device(): sum_squares = lax.psum(local_squares, 'people')  87.1 us
    dot_general x32, matrix products, per_device(): jnp.dot(state.astype(jnp.bfloat16), block_x, preferred_element_type=jnp.f...  60.1 us
    dot_general x32, matrix products, sample_block(): jnp.dot((summed_row + coupled).astype(jnp.bfloat16), block_basis, preferr...  54.1 us
  transfers between devices with their start and end apart: 32, of which 32 were waited for; matrix products, arithmetic and copies ran while one was open for 2% of the time, Pallas kernels for 0%

commit v1 on v0

--- a/solution.py
+++ b/solution.py
@@ -14,7 +14,7 @@
 
 
 def sum_block(stacked):
-    return lax.psum(stacked, "people")
+    return jnp.sum(lax.all_gather(stacked, "people"), axis=0)
 
 
 def sample_block(summed_row, old_effects, block_basis, block_eig, draws_block, spread, ridge):

time: 2380 us -> 1490 us (0.63)
  waiting for transfers between devices: 1990 us -> 109 us
  blocking collectives: 87.1 us -> 1090 us
    psum x28 -> x0, waiting for transfers between devices: 1860 us -> none  [sum_block(): return lax.psum(stacked, 'people')]
    all_gather x0 -> x32, blocking collectives: none -> 1000 us  [sum_block(): return jnp.sum(lax.all_gather(stacked, 'people'), axis=0)]
  transfers between devices with their start and end apart: 32 -> 4, of which waited for: 32 -> 4; matrix products, arithmetic and copies ran while one was open for 2% -> 0% of each run, Pallas kernels for 0% -> 0%
where the time goes in v1:
time: 1490 us; the launch traced here: 1480 us
  blocking collectives  1090 us (73%)
  matrix products  225 us (15%)
  waiting for transfers between devices  109 us (7%)
  between operations  35.4 us (2%)
    all_gather x32, blocking collectives, sum_block(): return jnp.sum(lax.all_gather(stacked, 'people'), axis=0)  1000 us
    psum x4, waiting for transfers between devices, per_device(): residual = start_residual + lax.psum(local_changes, 'snps')  109 us
    dot_general x64, matrix products, contract_last(): lax.dot_general(left, right, (((1,), (1,)), ((), ())), preferred_element_...  92.8 us
    psum x4, blocking collectives, per_device(): sum_squares = lax.psum(local_squares, 'people')  88.1 us
    dot_general x32, matrix products, sample_block(): jnp.dot((summed_row + coupled).astype(jnp.bfloat16), block_basis, preferr...  52.9 us
    dot_general x32, matrix products, sample_block(): jnp.dot(old_effects.astype(jnp.bfloat16), block_basis, preferred_element_...  39.8 us
    dot_general x32, matrix products, per_device(): jnp.dot(state.astype(jnp.bfloat16), block_x, preferred_element_type=jnp.f...  39.7 us
  transfers between devices with their start and end apart: 4, of which 4 were waited for; matrix products, arithmetic and copies ran while one was open for 0% of the time, Pallas kernels for 0%

profile of v1, /device:TPU:0, one launch (start us, length us, event | category | flops | bytes accessed | tf_op | source)
XLA Modules:
  0.0 1477.7 jit_solution(9015011138282662559)
XLA Ops:
  52.8 31.6 %all-gather = f32[256,512]{1,0:T(8,128)S(1)} all-gather(f32[32,512]{1,0:T(8,128)S(1)} %fusion.108), channel_id=2, replica_groups=mesh['people'=8,'snps'=4] {'people'}, dimensions={0}, use_global_device_ids=true | all-gather | bytes 589824 | tf_op jit(solution)/shard_map/all_gather | solution.py:17
  85.7 31.3 %all-gather.4 = f32[256,512]{1,0:T(8,128)S(1)} all-gather(f32[32,512]{1,0:T(8,128)S(1)} %fusion.109), channel_id=6, replica_groups=mesh['people'=8,'snps'=4] {'people'}, dimensions={0}, use_global_device_ids=true | all-gather | bytes 589824 | tf_op jit(solution)/shard_map/all_gather | solution.py:17
  127.0 31.5 %all-gather.1 = f32[256,512]{1,0:T(8,128)S(1)} all-gather(f32[32,512]{1,0:T(8,128)S(1)} %fusion.4), channel_id=3, replica_groups=mesh['people'=8,'snps'=4] {'people'}, dimensions={0}, use_global_device_ids=true | all-gather | bytes 589824 | tf_op jit(solution)/shard_map/all_gather | solution.py:17
  166.3 31.3 %all-gather.2 = f32[256,512]{1,0:T(8,128)S(1)} all-gather(f32[32,512]{1,0:T(8,128)S(1)} %fusion.7), channel_id=4, replica_groups=mesh['people'=8,'snps'=4] {'people'}, dimensions={0}, use_global_device_ids=true | all-gather | bytes 589824 | tf_op jit(solution)/shard_map/all_gather | solution.py:17
  205.3 31.6 %all-gather.3 = f32[256,512]{1,0:T(8,128)S(1)} all-gather(f32[32,512]{1,0:T(8,128)S(1)} %fusion.10), channel_id=5, replica_groups=mesh['people'=8,'snps'=4] {'people'}, dimensions={0}, use_global_device_ids=true | all-gather | bytes 589824 | tf_op jit(solution)/shard_map/all_gather | solution.py:17
  249.6 31.3 %all-gather.5 = f32[256,512]{1,0:T(8,128)S(1)} all-gather(f32[32,512]{1,0:T(8,128)S(1)} %fusion.14), channel_id=7, replica_groups=mesh['people'=8,'snps'=4] {'people'}, dimensions={0}, use_global_device_ids=true | all-gather | bytes 589824 | tf_op jit(solution)/shard_map/all_gather | solution.py:17
  288.6 31.4 %all-gather.6 = f32[256,512]{1,0:T(8,128)S(1)} all-gather(f32[32,512]{1,0:T(8,128)S(1)} %fusion.17), channel_id=8, replica_groups=mesh['people'=8,'snps'=4] {'people'}, dimensions={0}, use_global_device_ids=true | all-gather | bytes 589824 | tf_op jit(solution)/shard_map/all_gather | solution.py:17
  327.8 31.2 %all-gather.7 = f32[256,512]{1,0:T(8,128)S(1)} all-gather(f32[32,512]{1,0:T(8,128)S(1)} %fusion.20), channel_id=9, replica_groups=mesh['people'=8,'snps'=4] {'people'}, dimensions={0}, use_global_device_ids=true | all-gather | bytes 589824 | tf_op jit(solution)/shard_map/all_gather | solution.py:17
  421.3 31.5 %all-gather.8 = f32[256,512]{1,0:T(8,128)S(1)} all-gather(f32[32,512]{1,0:T(8,128)S(1)} %fusion.27), channel_id=10, replica_groups=mesh['people'=8,'snps'=4] {'people'}, dimensions={0}, use_global_device_ids=true | all-gather | bytes 589824 | tf_op jit(solution)/shard_map/all_gather | solution.py:17
  460.0 31.4 %all-gather.9 = f32[256,512]{1,0:T(8,128)S(1)} all-gather(f32[32,512]{1,0:T(8,128)S(1)} %fusion.30), channel_id=11, replica_groups=mesh['people'=8,'snps'=4] {'people'}, dimensions={0}, use_global_device_ids=true | all-gather | bytes 589824 | tf_op jit(solution)/shard_map/all_gather | solution.py:17
  498.5 31.4 %all-gather.10 = f32[256,512]{1,0:T(8,128)S(1)} all-gather(f32[32,512]{1,0:T(8,128)S(1)} %fusion.33), channel_id=12, replica_groups=mesh['people'=8,'snps'=4] {'people'}, dimensions={0}, use_global_device_ids=true | all-gather | bytes 589824 | tf_op jit(solution)/shard_map/all_gather | solution.py:17
  536.9 31.4 %all-gather.11 = f32[256,512]{1,0:T(8,128)S(1)} all-gather(f32[32,512]{1,0:T(8,128)S(1)} %fusion.36), channel_id=13, replica_groups=mesh['people'=8,'snps'=4] {'people'}, dimensions={0}, use_global_device_ids=true | all-gather | bytes 589824 | tf_op jit(solution)/shard_map/all_gather | solution.py:17
  572.7 31.6 %all-gather.12 = f32[256,512]{1,0:T(8,128)S(1)} all-gather(f32[32,512]{1,0:T(8,128)S(1)} %fusion.38), channel_id=14, replica_groups=mesh['people'=8,'snps'=4] {'people'}, dimensions={0}, use_global_device_ids=true | all-gather | bytes 589824 | tf_op jit(solution)/shard_map/all_gather | solution.py:17
  611.5 31.5 %all-gather.13 = f32[256,512]{1,0:T(8,128)S(1)} all-gather(f32[32,512]{1,0:T(8,128)S(1)} %fusion.41), channel_id=15, replica_groups=mesh['people'=8,'snps'=4] {'people'}, dimensions={0}, use_global_device_ids=true | all-gather | bytes 589824 | tf_op jit(solution)/shard_map/all_gather | solution.py:17
  650.1 31.2 %all-gather.14 = f32[256,512]{1,0:T(8,128)S(1)} all-gather(f32[32,512]{1,0:T(8,128)S(1)} %fusion.44), channel_id=16, replica_groups=mesh['people'=8,'snps'=4] {'people'}, dimensions={0}, use_global_device_ids=true | all-gather | bytes 589824 | tf_op jit(solution)/shard_map/all_gather | solution.py:17
  688.4 31.2 %all-gather.15 = f32[256,512]{1,0:T(8,128)S(1)} all-gather(f32[32,512]{1,0:T(8,128)S(1)} %fusion.47), channel_id=17, replica_groups=mesh['people'=8,'snps'=4] {'people'}, dimensions={0}, use_global_device_ids=true | all-gather | bytes 589824 | tf_op jit(solution)/shard_map/all_gather | solution.py:17
  778.9 31.5 %all-gather.16 = f32[256,512]{1,0:T(8,128)S(1)} all-gather(f32[32,512]{1,0:T(8,128)S(1)} %fusion.54), channel_id=18, replica_groups=mesh['people'=8,'snps'=4] {'people'}, dimensions={0}, use_global_device_ids=true | all-gather | bytes 589824 | tf_op jit(solution)/shard_map/all_gather | solution.py:17
  817.5 31.4 %all-gather.17 = f32[256,512]{1,0:T(8,128)S(1)} all-gather(f32[32,512]{1,0:T(8,128)S(1)} %fusion.57), channel_id=19, replica_groups=mesh['people'=8,'snps'=4] {'people'}, dimensions={0}, use_global_device_ids=true | all-gather | bytes 589824 | tf_op jit(solution)/shard_map/all_gather | solution.py:17
  856.0 31.4 %all-gather.18 = f32[256,512]{1,0:T(8,128)S(1)} all-gather(f32[32,512]{1,0:T(8,128)S(1)} %fusion.60), channel_id=20, replica_groups=mesh['people'=8,'snps'=4] {'people'}, dimensions={0}, use_global_device_ids=true | all-gather | bytes 589824 | tf_op jit(solution)/shard_map/all_gather | solution.py:17
  894.5 31.5 %all-gather.19 = f32[256,512]{1,0:T(8,128)S(1)} all-gather(f32[32,512]{1,0:T(8,128)S(1)} %fusion.63), channel_id=21, replica_groups=mesh['people'=8,'snps'=4] {'people'}, dimensions={0}, use_global_device_ids=true | all-gather | bytes 589824 | tf_op jit(solution)/shard_map/all_gather | solution.py:17
  930.4 31.6 %all-gather.20 = f32[256,512]{1,0:T(8,128)S(1)} all-gather(f32[32,512]{1,0:T(8,128)S(1)} %fusion.65), channel_id=22, replica_groups=mesh['people'=8,'snps'=4] {'people'}, dimensions={0}, use_global_device_ids=true | all-gather | bytes 589824 | tf_op jit(solution)/shard_map/all_gather | solution.py:17
  969.1 31.4 %all-gather.21 = f32[256,512]{1,0:T(8,128)S(1)} all-gather(f32[32,512]{1,0:T(8,128)S(1)} %fusion.68), channel_id=23, replica_groups=mesh['people'=8,'snps'=4] {'people'}, dimensions={0}, use_global_device_ids=true | all-gather | bytes 589824 | tf_op jit(solution)/shard_map/all_gather | solution.py:17
  1007.6 31.3 %all-gather.22 = f32[256,512]{1,0:T(8,128)S(1)} all-gather(f32[32,512]{1,0:T(8,128)S(1)} %fusion.71), channel_id=24, replica_groups=mesh['people'=8,'snps'=4] {'people'}, dimensions={0}, use_global_device_ids=true | all-gather | bytes 589824 | tf_op jit(solution)/shard_map/all_gather | solution.py:17
  1046.0 31.2 %all-gather.23 = f32[256,512]{1,0:T(8,128)S(1)} all-gather(f32[32,512]{1,0:T(8,128)S(1)} %fusion.74), channel_id=25, replica_groups=mesh['people'=8,'snps'=4] {'people'}, dimensions={0}, use_global_device_ids=true | all-gather | bytes 589824 | tf_op jit(solution)/shard_map/all_gather | solution.py:17
  1136.6 31.5 %all-gather.24 = f32[256,512]{1,0:T(8,128)S(1)} all-gather(f32[32,512]{1,0:T(8,128)S(1)} %fusion.81), channel_id=26, replica_groups=mesh['people'=8,'snps'=4] {'people'}, dimensions={0}, use_global_device_ids=true | all-gather | bytes 589824 | tf_op jit(solution)/shard_map/all_gather | solution.py:17
  1175.2 31.6 %all-gather.25 = f32[256,512]{1,0:T(8,128)S(1)} all-gather(f32[32,512]{1,0:T(8,128)S(1)} %fusion.84), channel_id=27, replica_groups=mesh['people'=8,'snps'=4] {'people'}, dimensions={0}, use_global_device_ids=true | all-gather | bytes 589824 | tf_op jit(solution)/shard_map/all_gather | solution.py:17
  1213.9 31.4 %all-gather.26 = f32[256,512]{1,0:T(8,128)S(1)} all-gather(f32[32,512]{1,0:T(8,128)S(1)} %fusion.87), channel_id=28, replica_groups=mesh['people'=8,'snps'=4] {'people'}, dimensions={0}, use_global_device_ids=true | all-gather | bytes 589824 | tf_op jit(solution)/shard_map/all_gather | solution.py:17
  1252.4 31.5 %all-gather.27 = f32[256,512]{1,0:T(8,128)S(1)} all-gather(f32[32,512]{1,0:T(8,128)S(1)} %fusion.90), channel_id=29, replica_groups=mesh['people'=8,'snps'=4] {'people'}, dimensions={0}, use_global_device_ids=true | all-gather | bytes 589824 | tf_op jit(solution)/shard_map/all_gather | solution.py:17
  1288.4 31.5 %all-gather.28 = f32[256,512]{1,0:T(8,128)S(1)} all-gather(f32[32,512]{1,0:T(8,128)S(1)} %fusion.92), channel_id=30, replica_groups=mesh['people'=8,'snps'=4] {'people'}, dimensions={0}, use_global_device_ids=true | all-gather | bytes 589824 | tf_op jit(solution)/shard_map/all_gather | solution.py:17
  1327.0 31.3 %all-gather.29 = f32[256,512]{1,0:T(8,128)S(1)} all-gather(f32[32,512]{1,0:T(8,128)S(1)} %fusion.95), channel_id=31, replica_groups=mesh['people'=8,'snps'=4] {'people'}, dimensions={0}, use_global_device_ids=true | all-gather | bytes 589824 | tf_op jit(solution)/shard_map/all_gather | solution.py:17
  1365.4 31.2 %all-gather.30 = f32[256,512]{1,0:T(8,128)S(1)} all-gather(f32[32,512]{1,0:T(8,128)S(1)} %fusion.98), channel_id=32, replica_groups=mesh['people'=8,'snps'=4] {'people'}, dimensions={0}, use_global_device_ids=true | all-gather | bytes 589824 | tf_op jit(solution)/shard_map/all_gather | solution.py:17
  1403.7 31.2 %all-gather.31 = f32[256,512]{1,0:T(8,128)S(1)} all-gather(f32[32,512]{1,0:T(8,128)S(1)} %fusion.101), channel_id=33, replica_groups=mesh['people'=8,'snps'=4] {'people'}, dimensions={0}, use_global_device_ids=true | all-gather | bytes 589824 | tf_op jit(solution)/shard_map/all_gather | solution.py:17
  (337 shorter events, 437.6 us)
Async XLA Ops:
  7.2 112.8 %copy-start.1 = (f32[32,4096]{1,0:T(8,128)S(1)}, f32[32,4096]{1,0:T(8,128)}, u32[]{:S(2)}) copy-start(f32[32,4096]{1,0:T(8,128)} %param.13) | copy-start | bytes 1572868
  7.2 110.5 %copy-start.3 = (bf16[4,32,4096]{2,1,0:T(8,128)(2,1)S(1)}, bf16[4,32,4096]{2,1,0:T(8,128)(2,1)}, u32[]{:S(2)}) copy-start(bf16[4,32,4096]{2,1,0:T(8,128)(2,1)} %param.20) | copy-start | bytes 3145732
  7.2 114.0 %copy-start.8 = (f32[32]{0:T(128)S(1)}, f32[32]{0:T(128)}, u32[]{:S(2)}) copy-start(f32[32]{0:T(128)} %param.18) | copy-start | bytes 388
  7.2 389.2 %all-reduce.5.cloned.1.call-start = ((), (), s32[]{:S(2)}) async-start(), calls=%async_computation | async-start | bytes 131072 | tf_op jit(solution)/shard_map/psum | solution.py:110
  50.5 67.1 %copy-start.21 = (f32[512]{0:T(512)}, f32[512]{0:T(512)S(1)}, u32[]{:S(2)}) copy-start(f32[512]{0:T(512)S(1)} %get-tuple-element.121) | copy-start | bytes 6148
  50.5 67.1 %copy-start.23 = (f32[512]{0:T(512)}, f32[512]{0:T(512)S(1)}, u32[]{:S(2)}) copy-start(f32[512]{0:T(512)S(1)} %get-tuple-element.113) | copy-start | bytes 6148
  51.5 71.4 %copy-start.2 = (f32[32,4096]{1,0:T(8,128)S(1)}, f32[32,4096]{1,0:T(8,128)}, u32[]{:S(2)}) copy-start(f32[32,4096]{1,0:T(8,128)} %param.13) | copy-start | bytes 1572868
  84.4 39.9 %copy-start = (f32[32,512]{1,0:T(8,128)S(1)}, f32[32,512]{1,0:T(8,128)}, u32[]{:S(2)}) copy-start(f32[32,512]{1,0:T(8,128)} %param.12) | copy-start | bytes 196612
  117.6 3.6 copy-start.9
  118.6 203.5 %copy-start.6 = (bf16[1,32,4096]{2,1,0:T(8,128)(2,1)}, bf16[1,32,4096]{2,1,0:T(8,128)(2,1)S(1)}, u32[]{:S(2)}) copy-start(bf16[1,32,4096]{2,1,0:T(8,128)(2,1)S(1)} %get-tuple-element.31) | copy-start | bytes 786436
  118.6 43.6 %copy-start.18 = (f32[512]{0:T(512)S(1)}, f32[512]{0:T(512)}, u32[]{:S(2)}) copy-start(f32[512]{0:T(512)} %get-tuple-element.120) | copy-start | bytes 6148
  122.9 42.2 %copy-start.17 = (f32[512]{0:T(512)S(1)}, f32[512]{0:T(512)}, u32[]{:S(2)}) copy-start(f32[512]{0:T(512)} %get-tuple-element.117) | copy-start | bytes 6148
  158.6 42.6 %copy-start.16 = (f32[512]{0:T(512)S(1)}, f32[512]{0:T(512)}, u32[]{:S(2)}) copy-start(f32[512]{0:T(512)} %get-tuple-element.118) | copy-start | bytes 6148
  162.1 42.0 %copy-start.15 = (f32[512]{0:T(512)S(1)}, f32[512]{0:T(512)}, u32[]{:S(2)}) copy-start(f32[512]{0:T(512)} %get-tuple-element.115) | copy-start | bytes 6148
  197.7 42.8 %copy-start.14 = (f32[512]{0:T(512)S(1)}, f32[512]{0:T(512)}, u32[]{:S(2)}) copy-start(f32[512]{0:T(512)} %get-tuple-element.116) | copy-start | bytes 6148
  204.1 41.4 %copy-start.13 = (f32[512]{0:T(512)S(1)}, f32[512]{0:T(512)}, u32[]{:S(2)}) copy-start(f32[512]{0:T(512)} %get-tuple-element.114) | copy-start | bytes 6148
  236.9 11.5 copy-start.12
  241.9 42.6 %copy-start.11 = (f32[512]{0:T(512)S(1)}, f32[512]{0:T(512)}, u32[]{:S(2)}) copy-start(f32[512]{0:T(512)} %get-tuple-element.124) | copy-start | bytes 6148
  245.5 41.9 %copy-start.10 = (f32[512]{0:T(512)S(1)}, f32[512]{0:T(512)}, u32[]{:S(2)}) copy-start(f32[512]{0:T(512)} %get-tuple-element.125) | copy-start | bytes 6148
  327.8 69.6 %copy-start.24 = (f32[512]{0:T(512)S(1)}, f32[512]{0:T(512)}, u32[]{:S(2)}) copy-start(f32[512]{0:T(512)} %copy-done.23) | copy-start | bytes 6148
  359.0 39.6 %copy-start.22 = (f32[512]{0:T(512)S(1)}, f32[512]{0:T(512)}, u32[]{:S(2)}) copy-start(f32[512]{0:T(512)} %copy-done.21) | copy-start | bytes 6148
  359.1 62.3 %copy-start.25 = (f32[32]{0:T(128)S(1)}, f32[32]{0:T(128)}, u32[]{:S(2)}) copy-start(f32[32]{0:T(128)} %param.19) | copy-start | bytes 388
  361.0 91.9 %copy-start.5 = (bf16[1,32,4096]{2,1,0:T(8,128)(2,1)S(1)}, bf16[1,32,4096]{2,1,0:T(8,128)(2,1)}, u32[]{:S(2)}) copy-start(bf16[1,32,4096]{2,1,0:T(8,128)(2,1)} %get-tuple-element.30) | copy-start | bytes 786436
  362.7 91.8 %copy-start.20 = (f32[512]{0:T(512)S(1)}, f32[512]{0:T(512)}, u32[]{:S(2)}) copy-start(f32[512]{0:T(512)} %get-tuple-element.122) | copy-start | bytes 6148
  367.5 386.6 %all-reduce.7.cloned.1.call-start = ((), (), s32[]{:S(2)}) async-start(), calls=%async_computation.1 | async-start | bytes 131072 | tf_op jit(solution)/shard_map/psum | solution.py:110
  368.8 89.9 %copy-start.19 = (f32[512]{0:T(512)S(1)}, f32[512]{0:T(512)}, u32[]{:S(2)}) copy-start(f32[512]{0:T(512)} %get-tuple-element.119) | copy-start | bytes 6148
  719.6 90.9 %copy-start.4 = (bf16[1,32,4096]{2,1,0:T(8,128)(2,1)S(1)}, bf16[1,32,4096]{2,1,0:T(8,128)(2,1)}, u32[]{:S(2)}) copy-start(bf16[1,32,4096]{2,1,0:T(8,128)(2,1)} %get-tuple-element.32) | copy-start | bytes 786436
  726.0 385.7 %all-reduce.9.cloned.1.call-start = ((), (), s32[]{:S(2)}) async-start(), calls=%async_computation.2 | async-start | bytes 131072 | tf_op jit(solution)/shard_map/psum | solution.py:110
  1083.6 386.1 %all-reduce.11.cloned.1.call-start = ((), (), s32[]{:S(2)}) async-start(), calls=%async_computation.3 | async-start | bytes 131072 | tf_op jit(solution)/shard_map/psum | solution.py:110
  1438.0 33.1 %copy-start.7 = (f32[32,4096]{1,0:T(8,128)}, f32[32,4096]{1,0:T(8,128)S(1)}, u32[]{:S(2)}) copy-start(f32[32,4096]{1,0:T(8,128)S(1)} %get-tuple-element.36) | copy-start | bytes 1572868
Sparse Core Ops, SparseCore 0:
  367.6 28.7 all-reduce.4
  726.1 27.8 all-reduce.6
  1083.8 27.9 all-reduce.8
  1441.7 27.9 all-reduce.10
